TPU v7x, 32 devices: a whole 2x2x4 slice. The times are simulated.
32 devices in a mesh: groups: 2 (over x), pairs: 16 (over z, y, core).
Axes of the slice: x: 2, y: 2, z: 4, core: 2. Of those that a mesh axis runs over, the one named last changes fastest.
Arguments:
- traces: bfloat16 [128, 3, 4096], P(('groups', 'pairs')), parts along dimension 0, may hold values from -6 to 6
- gaps: int32 [128, 2], P(('groups', 'pairs')), parts along dimension 0, may hold values 0 or 1
- assign: int32 [128], P('groups'), parts along dimension 0, may hold values from 0 to 3, as said below
- target: int32 [32], P('groups'), parts along dimension 0, may hold values from 0 to 3, as said below
Outputs:
- correlations: bfloat16 [128, 16, 2, 9, 256], P(('groups', 'pairs')), parts along dimension 0
- energy: float32 [128, 9], P(('groups', 'pairs')), parts along dimension 0
There are 2 independent parts, one for each index of `groups`. A program takes and returns all parts, laid end to end along the dimension named above; each array names one. Nothing has to cross between parts.
Inputs may be any that keep to these rules, and one draw needn't show every extreme that they name: `assign`: the 4 stations of one owner name at most 2 stations of any block; in every draw one block takes exactly 2 stations of every owner. `target`: in every draw some owner names the block that takes 2 stations of every owner.
All inputs are finite; a program needn't handle non-finite values. No bound on the sum of `gaps` on one device may be relied on, other than what follows from the above.
Results may differ from a plain program's by a relative error of at most 0.0075.
Values may be sent and summed in bfloat16 or wider, within the bound.
No kernel may reach another device: no remote copies, remote signals or barrier semaphores. Data moves between devices by JAX's collectives and lax.ppermute only.
A program may use at most 128 MiB of HBM per device.

v0:
```python
import math
import jax
import jax.numpy as jnp
from jax import lax
from jax.sharding import PartitionSpec as P

SEG = 2048
FREQ = 512
FLO = 64
LAGS = 256
HALF = 21
CAP = 2


def dft_table():
    samples = jnp.arange(SEG, dtype=jnp.int32)[:, None]
    bins = FLO + jnp.arange(FREQ, dtype=jnp.int32)[None, :]
    phase = jnp.mod(samples * bins, SEG).astype(jnp.float32) * (2.0 * math.pi / SEG)
    return jnp.concatenate([jnp.cos(phase), -jnp.sin(phase)], axis=1).astype(jnp.bfloat16)


def lag_table():
    bins = FLO + jnp.arange(FREQ, dtype=jnp.int32)[:, None]
    shifts = jnp.arange(LAGS, dtype=jnp.int32)[None, :] - LAGS // 2
    phase = jnp.mod(bins * shifts, SEG).astype(jnp.float32) * (2.0 * math.pi / SEG)
    return jnp.concatenate([jnp.cos(phase), -jnp.sin(phase)], axis=0).astype(jnp.bfloat16)


def smooth_band():
    column = jnp.arange(FREQ, dtype=jnp.int32)
    band = (jnp.abs(column[:, None] - column[None, :]) <= HALF).astype(jnp.float32)
    return (band, jnp.sum(band, axis=0))


def whiten_all(traces, gaps):
    stations = traces.shape[0]
    windows = gaps.shape[1]
    segments = traces.reshape(stations * 3 * windows, SEG)
    spectra = jnp.dot(segments, dft_table(), preferred_element_type=jnp.float32)
    spectra = spectra.reshape(stations, 3, windows, 2, FREQ)
    power = jnp.sum(spectra * spectra, axis=(1, 3)) / 3.0
    band, bin_count = smooth_band()
    smooth = jnp.dot(power.reshape(-1, FREQ), band, precision=lax.Precision.HIGHEST)
    smooth = smooth.reshape(stations, windows, FREQ) / bin_count
    factor = gaps.astype(jnp.float32)[:, :, None] / jnp.sqrt(smooth + 1e-06)
    return (spectra * factor[:, None, :, None, :]).astype(jnp.bfloat16)


def station_ranks(owner_assign):
    own_count = owner_assign.shape[1]
    same = owner_assign[:, :, None] == owner_assign[:, None, :]
    order = jnp.arange(own_count, dtype=jnp.int32)
    before = order[:, None] < order[None, :]
    return jnp.sum((same & before[None, :, :]).astype(jnp.int32), axis=1)


def correlate_block(whitened, own_mask, partner, partner_mask, lag_tab):
    own_count = whitened.shape[0]
    slot_count = partner.shape[0]
    real_part = partner[:, :, :, 0]
    imag_part = partner[:, :, :, 1]
    quad = jnp.stack(
        [jnp.stack([real_part, imag_part], 3), jnp.stack([-imag_part, real_part], 3)], 4
    )
    cross = jnp.einsum("icwrf,jdwrof->ijcdof", whitened, quad, preferred_element_type=jnp.float32)
    cross = cross.astype(jnp.bfloat16)
    lagged = jnp.dot(cross.reshape(-1, 2 * FREQ), lag_tab, preferred_element_type=jnp.float32)
    lagged = lagged.reshape(own_count, slot_count, 9, LAGS)
    counts = jnp.dot(own_mask, partner_mask.T, precision=lax.Precision.HIGHEST)
    scale = 1.0 / (jnp.maximum(counts, 1.0) * math.sqrt(FREQ))
    return (lagged * scale[:, :, None, None]).astype(jnp.bfloat16)


def correlate_slots(whitened, own_mask, partner, partner_mask):
    own_count = whitened.shape[0]
    windows = whitened.shape[2]
    senders = partner.shape[0]
    width = partner.shape[1]
    stride = min(senders, 16)
    lag_tab = lag_table()
    initial = jnp.zeros((own_count, senders, width, 9, LAGS), jnp.bfloat16)

    def advance(position, filled):
        start = position * stride
        piece = lax.dynamic_slice_in_dim(partner, start, stride, 0)
        piece = piece.reshape(stride * width, 3, windows, 2, FREQ)
        mask_piece = lax.dynamic_slice_in_dim(partner_mask, start, stride, 0)
        mask_piece = mask_piece.reshape(stride * width, windows).astype(jnp.float32)
        result = correlate_block(whitened, own_mask, piece, mask_piece, lag_tab)
        result = result.reshape(own_count, stride, width, 9, LAGS)
        return lax.dynamic_update_slice_in_dim(filled, result, start, 1)

    return lax.fori_loop(0, senders // stride, advance, initial)


def on_device(traces, gaps, assign, target):
    whitened = whiten_all(traces, gaps)
    own_count = whitened.shape[0]
    owners = lax.axis_size("pairs")
    my_index = lax.axis_index("pairs")
    own_mask = gaps.astype(jnp.float32)
    station_rows = whitened.reshape(own_count, -1)
    mask_rows = gaps.astype(jnp.bfloat16)
    owner_assign = assign.reshape(owners, own_count)
    ranks = station_ranks(owner_assign)
    slot_ids = jnp.arange(CAP, dtype=jnp.int32)
    wanted = lax.dynamic_index_in_dim(target, my_index, 0, keepdims=False)
    select_in = (
        (owner_assign == wanted)[:, None, :] & (ranks[:, None, :] == slot_ids[None, :, None])
    ).astype(jnp.bfloat16)
    my_assign = lax.dynamic_index_in_dim(owner_assign, my_index, 0, keepdims=False)
    my_ranks = lax.dynamic_index_in_dim(ranks, my_index, 0, keepdims=False)
    select_out = (
        (my_assign[None, :] == target[:, None])[:, None, :]
        & (my_ranks[None, None, :] == slot_ids[None, :, None])
    ).astype(jnp.bfloat16)
    everyone, every_mask = (
        lax.all_gather(station_rows, "pairs", axis=0, tiled=True),
        lax.all_gather(mask_rows, "pairs", axis=0, tiled=True),
    )
    partner = jnp.einsum(
        "ecs,esr->ecr",
        select_in,
        everyone.reshape(owners, own_count, -1),
        preferred_element_type=jnp.float32,
    ).astype(jnp.bfloat16)
    partner_mask = jnp.einsum(
        "ecs,esw->ecw",
        select_in,
        every_mask.reshape(owners, own_count, -1),
        preferred_element_type=jnp.float32,
    ).astype(jnp.bfloat16)
    correlations = correlate_slots(whitened, own_mask, partner, partner_mask)
    slot_energy = jnp.sum(jnp.square(correlations.astype(jnp.float32)), axis=(0, 4))
    returned = lax.all_to_all(slot_energy, "pairs", split_axis=0, concat_axis=0, tiled=True)
    energy = jnp.einsum(
        "pcs,pcq->sq", select_out.astype(jnp.float32), returned, precision=lax.Precision.HIGHEST
    )
    energy = energy / float(owners * LAGS)
    return (correlations, energy)


def solution(mesh):
    in_specs = (
        P(("groups", "pairs"), None, None),
        P(("groups", "pairs"), None),
        P("groups"),
        P("groups"),
    )
    out_specs = (P(("groups", "pairs"), None, None, None, None), P(("groups", "pairs"), None))
    return jax.shard_map(
        on_device, mesh=mesh, in_specs=in_specs, out_specs=out_specs, check_vma=False
    )
```

profile of v0, /device:TPU:0, one launch (start us, length us, event | category | flops | bytes accessed | tf_op | source)
XLA Modules:
  0.0 122.6 jit_solution(12688342774132318976)
XLA Ops:
  0.8 1.0 copy.74
  1.8 17.0 %cosine_convert_fusion = (bf16[2048,512]{1,0:T(8,128)(2,1)S(1)}, bf16[2048,512]{1,0:T(8,128)(2,1)S(1)}) fusion(s32[512]{0:T(512)S(1)} %iota_add_fusion), kind=kLoop, calls=%fused_computation.14 | loop fusion | flops 17825792 | bytes 4196352 | tf_op jit(solution)/shard_map/convert.2
  18.9 0.6 fusion.14
  19.9 0.6 dynamic_slice.17
  20.5 0.6 broadcast_compare_fusion
  22.0 25.5 %all-gather = bf16[16,4,6144]{2,1,0:T(4,128)(2,1)S(1)} all-gather(bf16[1,4,6144]{2,1,0:T(4,128)(2,1)S(1)} %fusion.31), channel_id=1, replica_groups=mesh['groups'=2,'pairs'=16] {'pairs'}, dimensions={0}, use_global_device_ids=true | all-gather | bytes 835584 | tf_op jit(solution)/shard_map/all_gather | solution.py:118
  47.5 0.6 convolution_convert_fusion
  49.1 17.4 %all-gather.1 = bf16[16,4,2]{1,2,0:T(2,128)(2,1)S(1)} all-gather(bf16[1,4,2]{1,2,0:T(2,128)(2,1)S(1)} %get-tuple-element.44), channel_id=1, replica_groups=mesh['groups'=2,'pairs'=16] {'pairs'}, dimensions={0}, use_global_device_ids=true | all-gather | bytes 272 | tf_op jit(solution)/shard_map/all_gather | solution.py:119
  66.7 0.8 fusion.22
  67.4 1.7 %copy.88 = bf16[4,3,2,2,512,1,1]{0,2,3,1,6,5,4:T(2,128)(2,1)S(1)} copy(bf16[4,3,2,2,512,1,1]{4,3,2,1,0,6,5:T(2,128)(2,1)S(1)} %fusion.32) | data formatting | bytes 98304 | tf_op jit(solution)/shard_map/convert_element_type | solution.py:46
  69.2 0.5 fusion.48
  69.9 0.8 pad_maximum_fusion
  70.7 3.5 %copy.79 = bf16[32,3,2,2,512]{0,2,3,1,4:T(2,128)(2,1)S(1)} copy(bf16[32,3,2,2,512]{4,0,3,2,1:T(8,128)(2,1)} %pad_maximum_fusion) | data formatting | bytes 786432 | tf_op jit(solution)/shard_map/while/body/eval_jaxpr/stack | solution.py:63
  74.2 3.1 %copy.80 = bf16[32,3,2,2,1,512]{0,2,3,4,1,5:T(2,128)(2,1)} copy(bf16[32,3,2,2,1,512]{5,3,2,1,0,4:T(2,128)(2,1)S(1)} %stack.20) | data formatting | bytes 786432 | tf_op jit(solution)/shard_map/while/body/eval_jaxpr/stack | solution.py:62
  77.3 11.5 %fusion = bf16[4,32,3,3,2,512]{1,0,2,4,3,5:T(4,128)(2,1)} fusion(bf16[4,3,2,2,512,1,1]{0,2,3,1,6,5,4:T(2,128)(2,1)S(1)} %copy.88, bf16[32,3,2,2,1,512]{0,2,3,4,1,5:T(2,128)(2,1)S(1)} %bitcast.54, bf16[32,3,2,2,1,512]{0,2,3,4,1,5:T(2,128)(2,1)} %copy.80), kind=kOutput, calls=%fused_computation.1 | convolution fusion | flops 12189696 | bytes 3194880 | tf_op jit(solution)/shard_map/while/body/eval_jaxpr/icwrf,jdwrof->ijcdof/dot_general | solution.py:65
  88.8 14.3 %copy.82 = bf16[4,32,3,3,2,512]{5,4,1,3,2,0:T(2,128)(2,1)S(1)} copy(bf16[4,32,3,3,2,512]{1,0,2,4,3,5:T(4,128)(2,1)} %fusion) | data formatting | bytes 4718592 | tf_op jit(solution)/shard_map/while/body/eval_jaxpr/convert_element_type | solution.py:66
  103.1 2.9 %dot_general.36 = bf16[4,32,9,1024]{3,1,2,0:T(8,128)(2,1)} reshape(bf16[4,32,3,3,2,512]{5,4,1,3,2,0:T(2,128)(2,1)S(1)} %copy.82) | data formatting | bytes 4718592 | tf_op jit(solution)/shard_map/while/body/eval_jaxpr/dot_general | solution.py:67
  106.1 2.5 %cosine_convert_fusion.1 = (bf16[512,256]{1,0:T(8,128)(2,1)S(1)}, bf16[512,256]{1,0:T(8,128)(2,1)S(1)}) fusion(s32[256]{0:T(256)S(1)} %copy-done, s32[512]{0:T(512)S(1)} %iota_add_fusion), kind=kLoop, calls=%fused_computation.51 | loop fusion | flops 2228224 | bytes 527360 | tf_op jit(solution)/shard_map/convert
  108.6 2.5 %multiply_reduce_fusion = (f32[32,9]{0,1:T(8,128)S(1)}, bf16[4,32,9,256]{3,1,2,0:T(8,128)(2,1)S(1)}) fusion(f32[4,32]{1,0:T(4,128)S(1)} %copy-done.5, bf16[4,32,9,1024]{3,1,2,0:T(8,128)(2,1)} %dot_general.36, bf16[512,256]{1,0:T(8,128)(2,1)S(1)} %get-tuple-element.41, bf16[512,256]{1,0:T(8,128)(2,1)S(1)} %get-tuple-element.40), kind=kOutput, calls=%fused_computation.23 | convolution fusion | flops 606502656 | bytes 3475072 | tf_op jit(solution)/shard_map/while/body/eval_jaxpr/dot_general | solution.py:67
  111.1 0.7 copy.84
  111.8 3.5 %all-to-all-start = ((f32[16,2,9]{2,1,0:T(2,128)}), f32[16,2,9]{2,1,0:T(2,128)S(1)}, u32[]{:S(2)}, u32[]{:S(2)}) async-start(f32[16,2,9]{2,1,0:T(2,128)} %bitcast.17), calls=%async_computation | async-start | bytes 32768 | tf_op jit(solution)/shard_map/all_to_all | solution.py:135
  115.8 1.2 copy.86
  117.0 4.7 %all-to-all-done = f32[16,2,9]{2,1,0:T(2,128)S(1)} async-done(((f32[16,2,9]{2,1,0:T(2,128)}), f32[16,2,9]{2,1,0:T(2,128)S(1)}, u32[]{:S(2)}, u32[]{:S(2)}) %all-to-all-start) | async-done | bytes 1184 | tf_op jit(solution)/shard_map/all_to_all | solution.py:135
  121.7 0.8 fusion.23
  (41 shorter events, 3.2 us)
Async XLA Ops:
  18.8 0.9 copy-start.1
  18.8 0.9 copy-start.2
  18.9 1.0 copy-start.3
  103.1 2.9 %copy-start = (s32[256]{0:T(256)S(1)}, s32[256]{0:T(256)}, u32[]{:S(2)}) copy-start(s32[256]{0:T(256)} %iota_add_fusion.1) | copy-start | bytes 3076
  103.1 5.4 %copy-start.5 = (f32[4,32]{1,0:T(4,128)S(1)}, f32[4,32]{1,0:T(4,128)}, u32[]{:S(2)}) copy-start(f32[4,32]{1,0:T(4,128)} %fusion.22) | copy-start | bytes 1540
  106.0 9.4 %copy-start.4 = (s32[16]{0:T(128)S(1)}, s32[16]{0:T(128)}, u32[]{:S(2)}) copy-start(s32[16]{0:T(128)} %param.7) | copy-start | bytes 196
  111.8 10.0 %all-to-all-start = ((f32[16,2,9]{2,1,0:T(2,128)}), f32[16,2,9]{2,1,0:T(2,128)S(1)}, u32[]{:S(2)}, u32[]{:S(2)}) async-start(f32[16,2,9]{2,1,0:T(2,128)} %bitcast.17), calls=%async_computation | async-start | bytes 32768 | tf_op jit(solution)/shard_map/all_to_all | solution.py:135
where the time goes:
time: 123 us
  blocking collectives  42.9 us (35%)
  local copies, waits for them, and re-layouts  31.3 us (25%)
  other arithmetic  21.9 us (18%)
  matrix products  17.3 us (14%)
  waiting for transfers between devices  4.73 us (4%)
  starting transfers between devices  3.49 us (3%)
    all_gather x1, blocking collectives, on_device(): lax.all_gather(station_rows, 'pairs', axis=0, tiled=True)  25.5 us
    another operation x2, other arithmetic  19.5 us
    all_gather x1, blocking collectives, on_device(): lax.all_gather(mask_rows, 'pairs', axis=0, tiled=True)  17.4 us
    convert_element_type x1, local copies, waits for them, and re-layouts, correlate_block(): cross = cross.astype(jnp.bfloat16)  14.3 us
    dot_general x1, matrix products, correlate_block(): jnp.einsum('icwrf,jdwrof->ijcdof', whitened, quad, preferred_element_type...  11.5 us
    all_to_all x1, waiting for transfers between devices, on_device(): lax.all_to_all(slot_energy, 'pairs', split_axis=0, concat_axis=0, tiled=T...  4.73 us
    another operation x1, local copies, waits for them, and re-layouts, correlate_block(): jnp.stack([-imag_part, real_part], 3)  3.52 us
    all_to_all x1, starting transfers between devices, on_device(): lax.all_to_all(slot_energy, 'pairs', split_axis=0, concat_axis=0, tiled=T...  3.49 us
  transfers between devices with their start and end apart: 1, of which 1 were waited for; matrix products, arithmetic and copies ran while one was open for 1% of the time, Pallas kernels for 0%

commit v1 on v0

--- a/solution.py
+++ b/solution.py
@@ -10,6 +10,19 @@
 LAGS = 256
 HALF = 21
 CAP = 2
+
+
+def ring_gather(x, axis, dim):
+    peers, index, rows = (lax.axis_size(axis), lax.axis_index(axis), x.shape[dim])
+    right = [(i, (i + 1) % peers) for i in range(peers)]
+    out = jnp.zeros((*x.shape[:dim], peers * rows, *x.shape[dim + 1 :]), x.dtype)
+    held = x
+    for step in range(peers):
+        holder = (index - step) % peers
+        out = lax.dynamic_update_slice_in_dim(out, held, holder * rows, axis=dim)
+        if step < peers - 1:
+            held = lax.ppermute(held, axis, right)
+    return out
 
 
 def dft_table():
@@ -116,7 +129,7 @@
     ).astype(jnp.bfloat16)
     everyone, every_mask = (
         lax.all_gather(station_rows, "pairs", axis=0, tiled=True),
-        lax.all_gather(mask_rows, "pairs", axis=0, tiled=True),
+        ring_gather(mask_rows, "pairs", 0),
     )
     partner = jnp.einsum(
         "ecs,esr->ecr",

time: 123 us -> 185 us (1.50)
  waiting for transfers between devices: 4.73 us -> 81.5 us
  blocking collectives: 42.9 us -> 24.8 us
    ppermute x0 -> x15, waiting for transfers between devices: none -> 76.5 us  [ring_gather(): held = lax.ppermute(held, axis, right)]
    all_gather x1 -> x0, blocking collectives: 17.4 us -> none  [on_device(): lax.all_gather(mask_rows, 'pairs', axis=0, tiled=True)]
    dynamic_update_slice x0 -> x16, local copies, waits for them, and re-layouts: none -> 3.01 us  [ring_gather(): out = lax.dynamic_update_slice_in_dim(out, held, holder * rows, axis=dim)]
    another operation x1, local copies, waits for them, and re-layouts: 3.52 us -> 1.54 us  [correlate_block(): jnp.stack([-imag_part, real_part], 3)]
  transfers between devices with their start and end apart: 1 -> 16, of which waited for: 1 -> 15; matrix products, arithmetic and copies ran while one was open for 1% -> 36% of each run, Pallas kernels for 0% -> 0%
where the time goes in v1:
time: 185 us; the launch traced here: 184 us
  waiting for transfers between devices  81.5 us (44%)
  local copies, waits for them, and re-layouts  31.4 us (17%)
  blocking collectives  24.8 us (13%)
  other arithmetic  22.6 us (12%)
  matrix products  18.4 us (10%)
  starting transfers between devices  4.49 us (2%)
    ppermute x15, waiting for transfers between devices, ring_gather(): held = lax.ppermute(held, axis, right)  76.5 us
    all_gather x1, blocking collectives, on_device(): lax.all_gather(station_rows, 'pairs', axis=0, tiled=True)  24.8 us
    another operation x2, other arithmetic  20.6 us
    convert_element_type x1, local copies, waits for them, and re-layouts, correlate_block(): cross = cross.astype(jnp.bfloat16)  14.3 us
    dot_general x1, matrix products, correlate_block(): jnp.einsum('icwrf,jdwrof->ijcdof', whitened, quad, preferred_element_type...  11.5 us
    all_to_all x1, waiting for transfers between devices, on_device(): lax.all_to_all(slot_energy, 'pairs', split_axis=0, concat_axis=0, tiled=T...  5 us
  transfers between devices with their start and end apart: 16, of which 15 were waited for; matrix products, arithmetic and copies ran while one was open for 36% of the time, Pallas kernels for 0%

profile of v1, /device:TPU:0, one launch (start us, length us, event | category | flops | bytes accessed | tf_op | source)
XLA Modules:
  0.0 184.2 jit_solution(6626903638414857391)
XLA Ops:
  2.0 18.2 %cosine_convert_fusion = (bf16[2048,512]{1,0:T(8,128)(2,1)S(1)}, bf16[2048,512]{1,0:T(8,128)(2,1)}) fusion(s32[512]{0:T(512)S(1)} %iota_add_fusion), kind=kLoop, calls=%fused_computation.14 | loop fusion | flops 17825792 | bytes 4196352 | tf_op jit(solution)/shard_map/convert.2
  25.0 24.8 %all-gather = bf16[16,4,6144]{2,1,0:T(4,128)(2,1)S(1)} all-gather(bf16[1,4,6144]{2,1,0:T(4,128)(2,1)S(1)} %fusion.31), channel_id=1, replica_groups=mesh['groups'=2,'pairs'=16] {'pairs'}, dimensions={0}, use_global_device_ids=true | all-gather | bytes 835584 | tf_op jit(solution)/shard_map/all_gather | solution.py:131
  53.5 3.1 %copy.85 = bf16[32,3,2,2,1,512]{0,2,3,4,1,5:T(2,128)(2,1)} copy(bf16[32,3,2,2,1,512]{5,3,2,1,0,4:T(2,128)(2,1)S(1)} %stack.20) | data formatting | bytes 786432 | tf_op jit(solution)/shard_map/while/body/eval_jaxpr/stack | solution.py:75
  58.3 11.5 %fusion = bf16[4,32,3,3,2,512]{1,0,2,4,3,5:T(4,128)(2,1)} fusion(bf16[4,3,2,2,512,1,1]{0,2,3,1,6,5,4:T(2,128)(2,1)S(1)} %copy.94, bf16[32,3,2,2,1,512]{0,2,3,4,1,5:T(2,128)(2,1)S(1)} %bitcast.53, bf16[32,3,2,2,1,512]{0,2,3,4,1,5:T(2,128)(2,1)} %copy.85), kind=kOutput, calls=%fused_computation.1 | convolution fusion | flops 12189696 | bytes 3194880 | tf_op jit(solution)/shard_map/while/body/eval_jaxpr/icwrf,jdwrof->ijcdof/dot_general | solution.py:78
  69.8 14.3 %copy.87 = bf16[4,32,3,3,2,512]{5,4,1,3,2,0:T(2,128)(2,1)S(1)} copy(bf16[4,32,3,3,2,512]{1,0,2,4,3,5:T(4,128)(2,1)} %fusion) | data formatting | bytes 4718592 | tf_op jit(solution)/shard_map/while/body/eval_jaxpr/convert_element_type | solution.py:79
  84.2 2.9 %dot_general.36 = bf16[4,32,9,1024]{3,1,2,0:T(8,128)(2,1)} reshape(bf16[4,32,3,3,2,512]{5,4,1,3,2,0:T(2,128)(2,1)S(1)} %copy.87) | data formatting | bytes 4718592 | tf_op jit(solution)/shard_map/while/body/eval_jaxpr/dot_general | solution.py:80
  87.0 2.5 %cosine_convert_fusion.1 = (bf16[512,256]{1,0:T(8,128)(2,1)S(1)}, bf16[512,256]{1,0:T(8,128)(2,1)S(1)}) fusion(s32[256]{0:T(256)S(1)} %iota_add_fusion.1, s32[512]{0:T(512)S(1)} %iota_add_fusion), kind=kLoop, calls=%fused_computation.51 | loop fusion | flops 2228224 | bytes 527360 | tf_op jit(solution)/shard_map/convert
  90.5 5.1 %collective-permute-done.1 = bf16[4,2]{0,1:T(2,128)(2,1)S(1)} collective-permute-done((bf16[4,2]{0,1:T(2,128)(2,1)S(1)}, bf16[4,2]{0,1:T(2,128)(2,1)S(1)}, u32[]{:S(2)}, u32[]{:S(2)}) %collective-permute-start.1) | collective-permute-done | bytes 48 | tf_op jit(solution)/shard_map/ppermute | solution.py:24
  95.8 5.5 %collective-permute-done.2 = bf16[4,2]{0,1:T(2,128)(2,1)S(1)} collective-permute-done((bf16[4,2]{0,1:T(2,128)(2,1)S(1)}, bf16[4,2]{0,1:T(2,128)(2,1)S(1)}, u32[]{:S(2)}, u32[]{:S(2)}) %collective-permute-start.2) | collective-permute-done | bytes 48 | tf_op jit(solution)/shard_map/ppermute | solution.py:24
  101.5 5.5 %collective-permute-done.3 = bf16[4,2]{0,1:T(2,128)(2,1)S(1)} collective-permute-done((bf16[4,2]{0,1:T(2,128)(2,1)S(1)}, bf16[4,2]{0,1:T(2,128)(2,1)S(1)}, u32[]{:S(2)}, u32[]{:S(2)}) %collective-permute-start.3) | collective-permute-done | bytes 48 | tf_op jit(solution)/shard_map/ppermute | solution.py:24
  107.1 5.5 %collective-permute-done.4 = bf16[4,2]{0,1:T(2,128)(2,1)S(1)} collective-permute-done((bf16[4,2]{0,1:T(2,128)(2,1)S(1)}, bf16[4,2]{0,1:T(2,128)(2,1)S(1)}, u32[]{:S(2)}, u32[]{:S(2)}) %collective-permute-start.4) | collective-permute-done | bytes 48 | tf_op jit(solution)/shard_map/ppermute | solution.py:24
  112.8 5.5 %collective-permute-done.5 = bf16[4,2]{0,1:T(2,128)(2,1)S(1)} collective-permute-done((bf16[4,2]{0,1:T(2,128)(2,1)S(1)}, bf16[4,2]{0,1:T(2,128)(2,1)S(1)}, u32[]{:S(2)}, u32[]{:S(2)}) %collective-permute-start.5) | collective-permute-done | bytes 48 | tf_op jit(solution)/shard_map/ppermute | solution.py:24
  118.5 5.5 %collective-permute-done.6 = bf16[4,2]{0,1:T(2,128)(2,1)S(1)} collective-permute-done((bf16[4,2]{0,1:T(2,128)(2,1)S(1)}, bf16[4,2]{0,1:T(2,128)(2,1)S(1)}, u32[]{:S(2)}, u32[]{:S(2)}) %collective-permute-start.6) | collective-permute-done | bytes 48 | tf_op jit(solution)/shard_map/ppermute | solution.py:24
  124.2 5.5 %collective-permute-done.7 = bf16[4,2]{0,1:T(2,128)(2,1)S(1)} collective-permute-done((bf16[4,2]{0,1:T(2,128)(2,1)S(1)}, bf16[4,2]{0,1:T(2,128)(2,1)S(1)}, u32[]{:S(2)}, u32[]{:S(2)}) %collective-permute-start.7) | collective-permute-done | bytes 48 | tf_op jit(solution)/shard_map/ppermute | solution.py:24
  129.9 5.5 %collective-permute-done.8 = bf16[4,2]{0,1:T(2,128)(2,1)S(1)} collective-permute-done((bf16[4,2]{0,1:T(2,128)(2,1)S(1)}, bf16[4,2]{0,1:T(2,128)(2,1)S(1)}, u32[]{:S(2)}, u32[]{:S(2)}) %collective-permute-start.8) | collective-permute-done | bytes 48 | tf_op jit(solution)/shard_map/ppermute | solution.py:24
  135.6 5.5 %collective-permute-done.9 = bf16[4,2]{0,1:T(2,128)(2,1)S(1)} collective-permute-done((bf16[4,2]{0,1:T(2,128)(2,1)S(1)}, bf16[4,2]{0,1:T(2,128)(2,1)S(1)}, u32[]{:S(2)}, u32[]{:S(2)}) %collective-permute-start.9) | collective-permute-done | bytes 48 | tf_op jit(solution)/shard_map/ppermute | solution.py:24
  141.3 5.5 %collective-permute-done.10 = bf16[4,2]{0,1:T(2,128)(2,1)S(1)} collective-permute-done((bf16[4,2]{0,1:T(2,128)(2,1)S(1)}, bf16[4,2]{0,1:T(2,128)(2,1)S(1)}, u32[]{:S(2)}, u32[]{:S(2)}) %collective-permute-start.10) | collective-permute-done | bytes 48 | tf_op jit(solution)/shard_map/ppermute | solution.py:24
  147.0 5.5 %collective-permute-done.11 = bf16[4,2]{0,1:T(2,128)(2,1)S(1)} collective-permute-done((bf16[4,2]{0,1:T(2,128)(2,1)S(1)}, bf16[4,2]{0,1:T(2,128)(2,1)S(1)}, u32[]{:S(2)}, u32[]{:S(2)}) %collective-permute-start.11) | collective-permute-done | bytes 48 | tf_op jit(solution)/shard_map/ppermute | solution.py:24
  152.7 5.5 %collective-permute-done.12 = bf16[4,2]{0,1:T(2,128)(2,1)S(1)} collective-permute-done((bf16[4,2]{0,1:T(2,128)(2,1)S(1)}, bf16[4,2]{0,1:T(2,128)(2,1)S(1)}, u32[]{:S(2)}, u32[]{:S(2)}) %collective-permute-start.12) | collective-permute-done | bytes 48 | tf_op jit(solution)/shard_map/ppermute | solution.py:24
  158.4 5.5 %collective-permute-done.13 = bf16[4,2]{0,1:T(2,128)(2,1)S(1)} collective-permute-done((bf16[4,2]{0,1:T(2,128)(2,1)S(1)}, bf16[4,2]{0,1:T(2,128)(2,1)S(1)}, u32[]{:S(2)}, u32[]{:S(2)}) %collective-permute-start.13) | collective-permute-done | bytes 48 | tf_op jit(solution)/shard_map/ppermute | solution.py:24
  164.1 5.5 %collective-permute-done.14 = bf16[4,2]{0,1:T(2,128)(2,1)S(1)} collective-permute-done((bf16[4,2]{0,1:T(2,128)(2,1)S(1)}, bf16[4,2]{0,1:T(2,128)(2,1)S(1)}, u32[]{:S(2)}, u32[]{:S(2)}) %collective-permute-start.14) | collective-permute-done | bytes 48 | tf_op jit(solution)/shard_map/ppermute | solution.py:24
  170.2 2.6 %multiply_reduce_fusion = (f32[32,9]{0,1:T(8,128)S(1)}, bf16[4,32,9,256]{3,1,2,0:T(8,128)(2,1)S(1)}) fusion(f32[4,32]{1,0:T(4,128)S(1)} %fusion.22, bf16[4,32,9,1024]{3,1,2,0:T(8,128)(2,1)} %dot_general.36, bf16[512,256]{1,0:T(8,128)(2,1)S(1)} %get-tuple-element.41, bf16[512,256]{1,0:T(8,128)(2,1)S(1)} %get-tuple-element.40), kind=kOutput, calls=%fused_computation.23 | convolution fusion | flops 606502656 | bytes 3475072 | tf_op jit(solution)/shard_map/while/body/eval_jaxpr/dot_general | solution.py:80
  173.4 3.5 %all-to-all-start = ((f32[16,2,9]{2,1,0:T(2,128)}), f32[16,2,9]{2,1,0:T(2,128)S(1)}, u32[]{:S(2)}, u32[]{:S(2)}) async-start(f32[16,2,9]{2,1,0:T(2,128)} %bitcast.16), calls=%async_computation | async-start | bytes 32768 | tf_op jit(solution)/shard_map/all_to_all | solution.py:148
  178.4 5.0 %all-to-all-done = f32[16,2,9]{2,1,0:T(2,128)S(1)} async-done(((f32[16,2,9]{2,1,0:T(2,128)}), f32[16,2,9]{2,1,0:T(2,128)S(1)}, u32[]{:S(2)}, u32[]{:S(2)}) %all-to-all-start) | async-done | bytes 1184 | tf_op jit(solution)/shard_map/all_to_all | solution.py:148
  (84 shorter events, 18.4 us)
Async XLA Ops:
  0.6 19.5 %copy-start = (bf16[4,3,4096]{2,0,1:T(4,128)(2,1)S(1)}, bf16[4,3,4096]{2,0,1:T(4,128)(2,1)}, u32[]{:S(2)}) copy-start(bf16[4,3,4096]{2,0,1:T(4,128)(2,1)} %param.4) | copy-start | bytes 294916
  1.4 88.4 %collective-permute-start = (bf16[4,2]{0,1:T(2,128)(2,1)S(1)}, bf16[4,2]{0,1:T(2,128)(2,1)S(1)}, u32[]{:S(2)}, u32[]{:S(2)}) collective-permute-start(bf16[4,2]{0,1:T(2,128)(2,1)S(1)} %get-tuple-element.44), channel_id=1, source_target_pairs={{0,1},{1,2},{2,3},{3,4},{4,5},{5,6},{6,7},{7,8},{8,9},{9,10},{10,1... | collective-permute-start | bytes 56 | tf_op jit(solution)/shard_map/ppermute | solution.py:24
  20.4 2.4 %copy-start.2 = (s32[64]{0:T(128)S(1)}, s32[64]{0:T(128)}, u32[]{:S(2)}) copy-start(s32[64]{0:T(128)} %param.6) | copy-start | bytes 772
  20.4 2.6 %copy-start.3 = (s32[16]{0:T(128)S(1)}, s32[16]{0:T(128)}, u32[]{:S(2)}) copy-start(s32[16]{0:T(128)} %param.7) | copy-start | bytes 196
  84.1 85.9 %copy-start.1 = (s32[4,2]{0,1:T(2,128)S(1)}, s32[4,2]{0,1:T(2,128)}, u32[]{:S(2)}) copy-start(s32[4,2]{0,1:T(2,128)} %param.5) | copy-start | bytes 100
  89.8 5.7 %collective-permute-start.1 = (bf16[4,2]{0,1:T(2,128)(2,1)S(1)}, bf16[4,2]{0,1:T(2,128)(2,1)S(1)}, u32[]{:S(2)}, u32[]{:S(2)}) collective-permute-start(bf16[4,2]{0,1:T(2,128)(2,1)S(1)} %collective-permute-done), channel_id=1, source_target_pairs={{0,1},{1,2},{2,3},{3,4},{4,5},{5,6},{6,7},{7,8},{8,9},{9,10},{10,1... | collective-permute-start | bytes 56 | tf_op jit(solution)/shard_map/ppermute | solution.py:24
  95.6 5.7 %collective-permute-start.2 = (bf16[4,2]{0,1:T(2,128)(2,1)S(1)}, bf16[4,2]{0,1:T(2,128)(2,1)S(1)}, u32[]{:S(2)}, u32[]{:S(2)}) collective-permute-start(bf16[4,2]{0,1:T(2,128)(2,1)S(1)} %collective-permute-done.1), channel_id=1, source_target_pairs={{0,1},{1,2},{2,3},{3,4},{4,5},{5,6},{6,7},{7,8},{8,9},{9,10},{10,1... | collective-permute-start | bytes 56 | tf_op jit(solution)/shard_map/ppermute | solution.py:24
  101.3 5.7 %collective-permute-start.3 = (bf16[4,2]{0,1:T(2,128)(2,1)S(1)}, bf16[4,2]{0,1:T(2,128)(2,1)S(1)}, u32[]{:S(2)}, u32[]{:S(2)}) collective-permute-start(bf16[4,2]{0,1:T(2,128)(2,1)S(1)} %collective-permute-done.2), channel_id=1, source_target_pairs={{0,1},{1,2},{2,3},{3,4},{4,5},{5,6},{6,7},{7,8},{8,9},{9,10},{10,1... | collective-permute-start | bytes 56 | tf_op jit(solution)/shard_map/ppermute | solution.py:24
  107.0 5.7 %collective-permute-start.4 = (bf16[4,2]{0,1:T(2,128)(2,1)S(1)}, bf16[4,2]{0,1:T(2,128)(2,1)S(1)}, u32[]{:S(2)}, u32[]{:S(2)}) collective-permute-start(bf16[4,2]{0,1:T(2,128)(2,1)S(1)} %collective-permute-done.3), channel_id=1, source_target_pairs={{0,1},{1,2},{2,3},{3,4},{4,5},{5,6},{6,7},{7,8},{8,9},{9,10},{10,1... | collective-permute-start | bytes 56 | tf_op jit(solution)/shard_map/ppermute | solution.py:24
  112.6 5.7 %collective-permute-start.5 = (bf16[4,2]{0,1:T(2,128)(2,1)S(1)}, bf16[4,2]{0,1:T(2,128)(2,1)S(1)}, u32[]{:S(2)}, u32[]{:S(2)}) collective-permute-start(bf16[4,2]{0,1:T(2,128)(2,1)S(1)} %collective-permute-done.4), channel_id=1, source_target_pairs={{0,1},{1,2},{2,3},{3,4},{4,5},{5,6},{6,7},{7,8},{8,9},{9,10},{10,1... | collective-permute-start | bytes 56 | tf_op jit(solution)/shard_map/ppermute | solution.py:24
  118.3 5.7 %collective-permute-start.6 = (bf16[4,2]{0,1:T(2,128)(2,1)S(1)}, bf16[4,2]{0,1:T(2,128)(2,1)S(1)}, u32[]{:S(2)}, u32[]{:S(2)}) collective-permute-start(bf16[4,2]{0,1:T(2,128)(2,1)S(1)} %collective-permute-done.5), channel_id=1, source_target_pairs={{0,1},{1,2},{2,3},{3,4},{4,5},{5,6},{6,7},{7,8},{8,9},{9,10},{10,1... | collective-permute-start | bytes 56 | tf_op jit(solution)/shard_map/ppermute | solution.py:24
  124.0 5.7 %collective-permute-start.7 = (bf16[4,2]{0,1:T(2,128)(2,1)S(1)}, bf16[4,2]{0,1:T(2,128)(2,1)S(1)}, u32[]{:S(2)}, u32[]{:S(2)}) collective-permute-start(bf16[4,2]{0,1:T(2,128)(2,1)S(1)} %collective-permute-done.6), channel_id=1, source_target_pairs={{0,1},{1,2},{2,3},{3,4},{4,5},{5,6},{6,7},{7,8},{8,9},{9,10},{10,1... | collective-permute-start | bytes 56 | tf_op jit(solution)/shard_map/ppermute | solution.py:24
  129.7 5.7 %collective-permute-start.8 = (bf16[4,2]{0,1:T(2,128)(2,1)S(1)}, bf16[4,2]{0,1:T(2,128)(2,1)S(1)}, u32[]{:S(2)}, u32[]{:S(2)}) collective-permute-start(bf16[4,2]{0,1:T(2,128)(2,1)S(1)} %collective-permute-done.7), channel_id=1, source_target_pairs={{0,1},{1,2},{2,3},{3,4},{4,5},{5,6},{6,7},{7,8},{8,9},{9,10},{10,1... | collective-permute-start | bytes 56 | tf_op jit(solution)/shard_map/ppermute | solution.py:24
  135.4 5.7 %collective-permute-start.9 = (bf16[4,2]{0,1:T(2,128)(2,1)S(1)}, bf16[4,2]{0,1:T(2,128)(2,1)S(1)}, u32[]{:S(2)}, u32[]{:S(2)}) collective-permute-start(bf16[4,2]{0,1:T(2,128)(2,1)S(1)} %collective-permute-done.8), channel_id=1, source_target_pairs={{0,1},{1,2},{2,3},{3,4},{4,5},{5,6},{6,7},{7,8},{8,9},{9,10},{10,1... | collective-permute-start | bytes 56 | tf_op jit(solution)/shard_map/ppermute | solution.py:24
  141.1 5.7 %collective-permute-start.10 = (bf16[4,2]{0,1:T(2,128)(2,1)S(1)}, bf16[4,2]{0,1:T(2,128)(2,1)S(1)}, u32[]{:S(2)}, u32[]{:S(2)}) collective-permute-start(bf16[4,2]{0,1:T(2,128)(2,1)S(1)} %collective-permute-done.9), channel_id=1, source_target_pairs={{0,1},{1,2},{2,3},{3,4},{4,5},{5,6},{6,7},{7,8},{8,9},{9,10},{10,1... | collective-permute-start | bytes 56 | tf_op jit(solution)/shard_map/ppermute | solution.py:24
  146.8 5.7 %collective-permute-start.11 = (bf16[4,2]{0,1:T(2,128)(2,1)S(1)}, bf16[4,2]{0,1:T(2,128)(2,1)S(1)}, u32[]{:S(2)}, u32[]{:S(2)}) collective-permute-start(bf16[4,2]{0,1:T(2,128)(2,1)S(1)} %collective-permute-done.10), channel_id=1, source_target_pairs={{0,1},{1,2},{2,3},{3,4},{4,5},{5,6},{6,7},{7,8},{8,9},{9,10},{10,1... | collective-permute-start | bytes 56 | tf_op jit(solution)/shard_map/ppermute | solution.py:24
  152.5 5.7 %collective-permute-start.12 = (bf16[4,2]{0,1:T(2,128)(2,1)S(1)}, bf16[4,2]{0,1:T(2,128)(2,1)S(1)}, u32[]{:S(2)}, u32[]{:S(2)}) collective-permute-start(bf16[4,2]{0,1:T(2,128)(2,1)S(1)} %collective-permute-done.11), channel_id=1, source_target_pairs={{0,1},{1,2},{2,3},{3,4},{4,5},{5,6},{6,7},{7,8},{8,9},{9,10},{10,1... | collective-permute-start | bytes 56 | tf_op jit(solution)/shard_map/ppermute | solution.py:24
  158.2 5.7 %collective-permute-start.13 = (bf16[4,2]{0,1:T(2,128)(2,1)S(1)}, bf16[4,2]{0,1:T(2,128)(2,1)S(1)}, u32[]{:S(2)}, u32[]{:S(2)}) collective-permute-start(bf16[4,2]{0,1:T(2,128)(2,1)S(1)} %collective-permute-done.12), channel_id=1, source_target_pairs={{0,1},{1,2},{2,3},{3,4},{4,5},{5,6},{6,7},{7,8},{8,9},{9,10},{10,1... | collective-permute-start | bytes 56 | tf_op jit(solution)/shard_map/ppermute | solution.py:24
  163.9 5.7 %collective-permute-start.14 = (bf16[4,2]{0,1:T(2,128)(2,1)S(1)}, bf16[4,2]{0,1:T(2,128)(2,1)S(1)}, u32[]{:S(2)}, u32[]{:S(2)}) collective-permute-start(bf16[4,2]{0,1:T(2,128)(2,1)S(1)} %collective-permute-done.13), channel_id=1, source_target_pairs={{0,1},{1,2},{2,3},{3,4},{4,5},{5,6},{6,7},{7,8},{8,9},{9,10},{10,1... | collective-permute-start | bytes 56 | tf_op jit(solution)/shard_map/ppermute | solution.py:24
  173.4 10.0 %all-to-all-start = ((f32[16,2,9]{2,1,0:T(2,128)}), f32[16,2,9]{2,1,0:T(2,128)S(1)}, u32[]{:S(2)}, u32[]{:S(2)}) async-start(f32[16,2,9]{2,1,0:T(2,128)} %bitcast.16), calls=%async_computation | async-start | bytes 32768 | tf_op jit(solution)/shard_map/all_to_all | solution.py:148
